TPU v7x, 32 devices: a whole 2x2x4 slice. The times are simulated.
32 devices in a mesh: px: 8 (over z, x), py: 4 (over y, core).
Axes of the slice: x: 2, y: 2, z: 4, core: 2. Of those that a mesh axis runs over, the one named last changes fastest.
Arguments:
- particles: float32 [32, 2, 2, 128, 128], P(('px', 'py')), may hold values from -11 to 11
- orientation: int32 [32], P(('px', 'py')), may hold values from 0 to 7
- wedge_index: int32 [32], P(('px', 'py')), may hold values from 0 to 3
- half_set: int32 [32], P(('px', 'py')), may hold values from 0 to 1
- shell_map: int32 [2, 256, 256], P(None, ('px', 'py')), may hold values from 0 to 31, as said below
Outputs:
- half_maps: float32 [2, 2, 2, 256, 256], P(None, None, None, ('px', 'py'))
- fsc: float32 [32], replicated
Inputs may be any that keep to these rules, and one draw needn't show every extreme that they name: `shell_map`: every shell number occurs in every draw.
All inputs are finite; a program needn't handle non-finite values.
Results may differ from a plain program's by a relative error of at most 0.0003.
Values sent between devices are 32-bit elements; how exact they have to be, the bound alone decides.
No kernel may reach another device: no remote copies, remote signals or barrier semaphores. Data moves between devices by JAX's collectives and lax.ppermute only.
A program may use at most 64 MiB of HBM per device.

v0:
```python
import math

import jax
import jax.numpy as jnp
from jax import lax
from jax.sharding import PartitionSpec as P

NSHELL = 32


wedge_rise = (1, 3, 2, 3)
wedge_run = (1, 2, 1, 1)
sign_first = (1.0, -1.0, -1.0, 1.0, 1.0, -1.0, -1.0, 1.0)
sign_second = (1.0, 1.0, -1.0, -1.0, -1.0, -1.0, 1.0, 1.0)
highest = lax.Precision.HIGHEST


def select(lookup, position):
    entries = jnp.array(lookup)
    return jnp.sum(jnp.where(jnp.arange(len(lookup)) == position, entries, jnp.zeros_like(entries)))


def angle_table(sources, targets, extent):
    phases = sources[:, None] * targets[None, :] % extent
    angles = phases.astype(jnp.float32) * (2.0 * math.pi / extent)
    factor = 1.0 / math.sqrt(extent)
    return (jnp.cos(angles) * factor, jnp.sin(angles) * factor)


def coverage(plane_abs, spectral_abs, wedge_id):
    rise_value = select(wedge_rise, wedge_id)
    run_value = select(wedge_run, wedge_id)
    return (plane_abs[:, None] * run_value <= spectral_abs[None, :] * rise_value).astype(
        jnp.float32
    )


def shards(particles, orientation, wedge_index, half_set, shell_map):
    planes = particles.shape[2]
    box_side = particles.shape[3]
    extent = shell_map.shape[2]
    own_rows = shell_map.shape[1]
    plane_abs = jnp.abs((jnp.arange(planes, dtype=jnp.int32) - planes // 2) * (extent // planes))
    spectral = jnp.arange(extent, dtype=jnp.int32)
    spectral_abs = jnp.minimum(spectral, extent - spectral)
    cos_fwd, sin_fwd = angle_table(
        jnp.arange(box_side, dtype=jnp.int32) - box_side // 2, spectral, extent
    )
    totals = jnp.zeros((2, 2, planes, extent, extent), jnp.float32)
    source = particles[0]
    turn_index = orientation[0]
    swapped = turn_index % 2 == 1
    source = jnp.where(turn_index >= 4, jnp.roll(jnp.flip(source, 1), 1, 1), source)
    source = jnp.where(swapped, jnp.swapaxes(source, 2, 3), source)
    sign_outer = select(sign_first, turn_index)
    sign_inner = select(sign_second, turn_index)
    along_cos = jnp.einsum("czab,bk->czak", source, cos_fwd, precision=highest)
    along_sin = jnp.einsum("czab,bk->czak", source, sin_fwd, precision=highest)
    partial_turn = jnp.stack(
        [along_cos[0] + sign_inner * along_sin[1], along_cos[1] - sign_inner * along_sin[0]]
    )
    outer_cos = jnp.einsum("czak,aj->czjk", partial_turn, cos_fwd, precision=highest)
    outer_sin = jnp.einsum("czak,aj->czjk", partial_turn, sin_fwd, precision=highest)
    spectrum = jnp.stack(
        [outer_cos[0] + sign_outer * outer_sin[1], outer_cos[1] - sign_outer * outer_sin[0]]
    )
    covered = coverage(plane_abs, spectral_abs, wedge_index[0])
    covered = jnp.where(swapped, covered[:, None, :], covered[:, :, None])
    half_id = half_set[0]
    current = lax.dynamic_index_in_dim(totals, half_id, 0, False)
    totals = lax.dynamic_update_index_in_dim(totals, current + spectrum * covered, half_id, 0)
    reduced = lax.psum_scatter(totals, ("px", "py"), scatter_dimension=3, tiled=True)
    half_hot = (half_set[:, None] == jnp.arange(2)).astype(jnp.float32)
    wedge_hot = (wedge_index[:, None] == jnp.arange(4)).astype(jnp.float32)
    parity_hot = (orientation[:, None] % 2 == jnp.arange(2)).astype(jnp.float32)
    local_counts = jnp.einsum("ph,pw,pq->hwq", half_hot, wedge_hot, parity_hot, precision=highest)
    class_totals = lax.psum(local_counts, ("px", "py"))
    row_abs = lax.dynamic_slice_in_dim(
        spectral_abs, lax.axis_index(("px", "py")) * own_rows, own_rows
    )
    row_cover = jnp.stack([coverage(plane_abs, row_abs, wedge_id) for wedge_id in range(4)])
    column_cover = jnp.stack([coverage(plane_abs, spectral_abs, wedge_id) for wedge_id in range(4)])
    by_rows = jnp.einsum("hw,wzt->hzt", class_totals[:, :, 0], row_cover, precision=highest)
    by_columns = jnp.einsum("hw,wzk->hzk", class_totals[:, :, 1], column_cover, precision=highest)
    cover = by_rows[:, :, :, None] + by_columns[:, :, None, :]
    average = reduced / jnp.maximum(cover, 1.0)[:, None]
    cross = average[0, 0] * average[1, 0] + average[0, 1] * average[1, 1]
    power_first = average[0, 0] * average[0, 0] + average[0, 1] * average[0, 1]
    power_second = average[1, 0] * average[1, 0] + average[1, 1] * average[1, 1]
    stacked = jnp.stack([cross, power_first, power_second]).reshape(3, -1)
    membership = (shell_map.reshape(-1)[:, None] == jnp.arange(NSHELL)).astype(jnp.float32)
    shell_part = jnp.dot(stacked, membership, precision=highest)
    shell_total = lax.psum(shell_part, ("px", "py"))
    fsc = shell_total[0] / (jnp.sqrt(shell_total[1] * shell_total[2]) + 1e-06)
    n_rows = lax.axis_size("px")
    n_columns = lax.axis_size("py")
    cos_y, sin_y = angle_table(spectral, spectral, extent)
    middle_cos = jnp.einsum("hcztk,kp->hczpt", average, cos_y, precision=highest)
    middle_sin = jnp.einsum("hcztk,kp->hczpt", average, sin_y, precision=highest)
    middle = jnp.stack(
        [middle_cos[:, 0] - middle_sin[:, 1], middle_sin[:, 0] + middle_cos[:, 1]], axis=1
    )
    arrived = lax.all_to_all(
        lax.all_to_all(middle, "px", split_axis=3, concat_axis=4, tiled=True),
        "py",
        split_axis=3,
        concat_axis=4,
        tiled=True,
    )
    x_slot = spectral // own_rows
    x_source = (x_slot % n_rows * n_columns + x_slot // n_rows) * own_rows + spectral % own_rows
    cos_x, sin_x = angle_table(x_source, spectral, extent)
    final_cos = jnp.einsum("hczym,mx->hczyx", arrived, cos_x, precision=highest)
    final_sin = jnp.einsum("hczym,mx->hczyx", arrived, sin_x, precision=highest)
    half_maps = jnp.stack(
        [final_cos[:, 0] - final_sin[:, 1], final_sin[:, 0] + final_cos[:, 1]], axis=1
    )
    return (half_maps, fsc)


def solution(mesh):
    placed = (
        P(("px", "py"), None, None, None, None),
        P(("px", "py")),
        P(("px", "py")),
        P(("px", "py")),
        P(None, ("px", "py"), None),
    )
    return jax.shard_map(
        shards,
        mesh=mesh,
        in_specs=placed,
        out_specs=(P(None, None, None, ("px", "py"), None), P()),
        check_vma=False,
    )
```

profile of v0, /device:TPU:0, one launch (start us, length us, event | category | flops | bytes accessed | tf_op | source)
XLA Modules:
  0.0 240.1 jit_solution(11886774212349079399)
XLA Ops:
  7.9 1.1 copy.50
  9.0 2.0 fusion.38
  11.0 2.0 fusion.42
  14.5 1.5 convolution_bitcast_fusion.1
  16.0 1.5 convolution_bitcast_fusion
  18.1 0.8 fusion.81
  21.2 1.6 fusion.4
  23.0 0.9 copy-done.1
  24.0 1.3 copy-done
  25.6 42.0 %psum.14 = f32[2,4,2]{1,0,2:T(2,128)S(1)} all-reduce(f32[2,4,2]{1,0,2:T(2,128)S(1)} %multiply_bitcast_fusion), channel_id=1, replica_groups=mesh['px'=8,'py'=4] {'px','py'}, use_global_device_ids=true, to_apply=%region_5.6 | all-reduce | flops 16 | bytes 128 | tf_op jit(solution)/shard_map/psum | solution.py:77
  70.9 1.9 broadcast_multiply_fusion.10
  76.5 89.9 %reduce-scatter.2.cloned.1.call-done = f32[2,2,2,8,256]{4,3,2,1,0:T(8,128)} async-done(((f32[2,2,2,256,256]{4,3,2,1,0:T(8,128)}), f32[2,2,2,8,256]{4,3,2,1,0:T(8,128)}) %reduce-scatter.2.cloned.1.call-update) | async-done | bytes 65552 | tf_op jit(solution)/shard_map/reduce_scatter | solution.py:72
  166.4 0.8 broadcast_divide_fusion
  167.3 1.3 convolution_bitcast_fusion.2
  168.6 1.3 convolution_bitcast_fusion.3
  170.7 2.2 reshape.771
  173.0 3.4 %all-to-all-start = ((f32[8,1,2048]{2,1,0:T(1,128)}), f32[8,1,2048]{2,1,0:T(1,128)S(1)}, u32[]{:S(2)}, u32[]{:S(2)}) async-start(f32[8,1,2048]{2,1,0:T(1,128)} %reshape.771), calls=%async_computation.1 | async-start | bytes 131072 | tf_op jit(solution)/shard_map/all_to_all | solution.py:104
  176.7 39.8 %psum.15 = f32[3,32]{1,0:T(4,128)S(1)} all-reduce(f32[3,32]{1,0:T(4,128)S(1)} %fusion.5), channel_id=1, replica_groups=mesh['px'=8,'py'=4] {'px','py'}, use_global_device_ids=true, to_apply=%region_22.23 | all-reduce | flops 96 | bytes 768 | tf_op jit(solution)/shard_map/psum | solution.py:93
  218.0 1.6 reshape.772
  221.1 3.5 %all-to-all-start.1 = ((f32[4,1,4096]{2,1,0:T(1,128)}), f32[4,1,4096]{2,1,0:T(1,128)S(1)}, u32[]{:S(2)}, u32[]{:S(2)}) async-start(f32[4,1,4096]{2,1,0:T(1,128)} %reshape.773), calls=%async_computation.2 | async-start | bytes 131072 | tf_op jit(solution)/shard_map/all_to_all | solution.py:103
  225.2 3.6 %all-to-all-done.1 = f32[4,1,4096]{2,1,0:T(1,128)S(1)} async-done(((f32[4,1,4096]{2,1,0:T(1,128)}), f32[4,1,4096]{2,1,0:T(1,128)S(1)}, u32[]{:S(2)}, u32[]{:S(2)}) %all-to-all-start.1) | async-done | bytes 65568 | tf_op jit(solution)/shard_map/all_to_all | solution.py:103
  228.8 0.9 reduce.1
  230.0 1.3 fusion.14
  231.3 1.3 fusion.16
  (74 shorter events, 16.1 us)
Async XLA Ops:
  7.2 5.9 %copy-start.3 = (f32[8]{0:T(128)S(1)}, f32[8]{0:T(128)}, u32[]{:S(2)}) copy-start(f32[8]{0:T(128)} %constant.153.clone) | copy-start | bytes 100
  7.2 5.9 %copy-start.4 = (f32[8]{0:T(128)S(1)}, f32[8]{0:T(128)}, u32[]{:S(2)}) copy-start(f32[8]{0:T(128)} %constant.154.clone) | copy-start | bytes 100
  7.2 159.2 %reduce-scatter.2.cloned.1.call-start = ((), (), s32[]{:S(2)}) async-start(), calls=%async_computation.3 | async-start | bytes 2162688 | tf_op jit(solution)/shard_map/reduce_scatter | solution.py:72
  13.8 4.3 %copy-start.5 = (s32[4]{0:T(128)S(1)}, s32[4]{0:T(128)}, u32[]{:S(2)}) copy-start(s32[4]{0:T(128)} %constant.155.clone) | copy-start | bytes 52
  13.8 4.3 %copy-start.6 = (s32[4]{0:T(128)S(1)}, s32[4]{0:T(128)}, u32[]{:S(2)}) copy-start(s32[4]{0:T(128)} %constant.156.clone) | copy-start | bytes 52
  22.8 1.0 copy-start.1
  23.9 52.5 %copy-start.2 = (s32[2,8,256]{2,1,0:T(8,128)S(1)}, s32[2,8,256]{2,1,0:T(8,128)}, u32[]{:S(2)}) copy-start(s32[2,8,256]{2,1,0:T(8,128)} %param.29) | copy-start | bytes 49156
  24.0 1.4 copy-start
  173.0 43.6 %all-to-all-start = ((f32[8,1,2048]{2,1,0:T(1,128)}), f32[8,1,2048]{2,1,0:T(1,128)S(1)}, u32[]{:S(2)}, u32[]{:S(2)}) async-start(f32[8,1,2048]{2,1,0:T(1,128)} %reshape.771), calls=%async_computation.1 | async-start | bytes 131072 | tf_op jit(solution)/shard_map/all_to_all | solution.py:104
  221.1 7.7 %all-to-all-start.1 = ((f32[4,1,4096]{2,1,0:T(1,128)}), f32[4,1,4096]{2,1,0:T(1,128)S(1)}, u32[]{:S(2)}, u32[]{:S(2)}) async-start(f32[4,1,4096]{2,1,0:T(1,128)} %reshape.773), calls=%async_computation.2 | async-start | bytes 131072 | tf_op jit(solution)/shard_map/all_to_all | solution.py:103
Sparse Core Ops, SparseCore 0:
  25.5 140.9 reduce-scatter.1
where the time goes:
time: 241 us; the launch traced here: 240 us
  waiting for transfers between devices  93.5 us (39%)
  blocking collectives  81.8 us (34%)
  other arithmetic  18 us (7%)
  between operations  16.4 us (7%)
  matrix products  12.8 us (5%)
  local copies, waits for them, and re-layouts  10.6 us (4%)
  starting transfers between devices  6.93 us (3%)
    reduce_scatter x1, waiting for transfers between devices, shards(): lax.psum_scatter(totals, ('px', 'py'), scatter_dimension=3, tiled=True)  89.9 us
    psum x1, blocking collectives, shards(): class_totals = lax.psum(local_counts, ('px', 'py'))  42 us
    psum x1, blocking collectives, shards(): shell_total = lax.psum(shell_part, ('px', 'py'))  39.8 us
    unnamed x22, local copies, waits for them, and re-layouts  7.03 us
    mul x7, other arithmetic, coverage(): spectral_abs[None, :] * rise_value  6 us
  transfers between devices with their start and end apart: 3, of which 2 were waited for; matrix products, arithmetic and copies ran while one was open for 4% of the time, Pallas kernels for 0%

commit v1 on v0

--- a/solution.py
+++ b/solution.py
@@ -1,8 +1,12 @@
+import functools
 import math
 
 import jax
 import jax.numpy as jnp
+import numpy as np
 from jax import lax
+from jax.experimental import pallas as pl
+from jax.experimental.pallas import tpu as pltpu
 from jax.sharding import PartitionSpec as P
 
 NSHELL = 32
@@ -13,6 +17,406 @@
 sign_first = (1.0, -1.0, -1.0, 1.0, 1.0, -1.0, -1.0, 1.0)
 sign_second = (1.0, 1.0, -1.0, -1.0, -1.0, -1.0, 1.0, 1.0)
 highest = lax.Precision.HIGHEST
+axes = ("px", "py")
+
+SUBLANES = 8
+LANES = 128
+NWEDGE = len(wedge_rise)
+NCLASS = 1 + NWEDGE
+NSLOT = 2 * NCLASS
+ROW_LANE = 32
+
+
+def split_table(table):
+    high = table.astype(jnp.bfloat16)
+    low = (table - high.astype(np.float64)).astype(jnp.bfloat16)
+    return high, low
+
+
+def cos_sin(sources, targets, extent):
+    phases = np.outer(sources, targets) % extent
+    angles = phases * (2.0 * math.pi / extent)
+    factor = 1.0 / math.sqrt(extent)
+    return np.cos(angles) * factor, np.sin(angles) * factor
+
+
+def split(values):
+    high = values.astype(jnp.bfloat16)
+    low = (values - high.astype(jnp.float32)).astype(jnp.bfloat16)
+    return high, low
+
+
+def matmul(left, right, contract=((1,), (0,))):
+    return lax.dot_general(left, right, (contract, ((), ())), preferred_element_type=jnp.float32)
+
+
+def matmul_split(left, right, contract=((1,), (0,))):
+    return (
+        matmul(left[1], right[0], contract)
+        + matmul(left[0], right[1], contract)
+        + matmul(left[0], right[0], contract)
+    )
+
+
+def pick(lookup, position):
+    value = jnp.int32(lookup[0])
+    for entry in range(1, len(lookup)):
+        value = jnp.where(position == entry, jnp.int32(lookup[entry]), value)
+    return value
+
+
+def iota(shape, dimension):
+    return lax.broadcasted_iota(jnp.int32, shape, dimension)
+
+
+def spread_kernel(rows, turn_ref, wedge_ref, half_ref, source_ref, high_ref, low_ref, out_ref):
+    planes = source_ref.shape[2]
+    box_side = source_ref.shape[3]
+    extent = high_ref.shape[0]
+    devices = extent // rows
+    stride = out_ref.shape[0] // devices
+    turn = turn_ref[0]
+    wedge = wedge_ref[0]
+    half = half_ref[0]
+    swapped = (turn & 1) == 1
+    first = jnp.where(((turn + 1) & 2) == 2, -1.0, 1.0)
+    second = jnp.where(((turn + 2) & 4) == 4, -1.0, 1.0)
+    rise = pick(wedge_rise, wedge)
+    run = pick(wedge_run, wedge)
+    plane_abs = [abs(plane - planes // 2) * (extent // planes) for plane in range(planes)]
+
+    sign = jnp.full((1, box_side), first, jnp.float32).astype(jnp.bfloat16)
+    table = []
+    for ref in (high_ref, low_ref):
+        table.append(jnp.concatenate([ref[:, :box_side], ref[:, box_side:] * sign], axis=1))
+
+    def operand(axis):
+        parts = ([], [])
+        for plane in range(planes):
+            mirrored = (planes - plane) % planes
+            if mirrored == plane:
+                chosen = plane
+            else:
+                chosen = jnp.where(turn >= 4, mirrored, plane)
+            real = split(source_ref[0, 0, chosen])
+            imag = split(source_ref[0, 1, chosen])
+            for part in range(2):
+                parts[part].append(jnp.concatenate([real[part], imag[part]], axis=axis))
+                parts[part].append(jnp.concatenate([imag[part], -real[part]], axis=axis))
+        return [jnp.concatenate(part, axis=1 - axis) for part in parts]
+
+    def store(product, kept):
+        for plane in range(planes):
+            for part in range(2):
+                column = (plane * 2 + part) * box_side
+                block = product[:, column : column + box_side]
+                if kept is not None and plane_abs[plane] != 0:
+                    block = jnp.where(plane_abs[plane] * run <= kept * rise, block, 0.0)
+                for device in range(devices):
+                    start = device * stride + (part * planes + plane) * rows
+                    out_ref[start : start + rows, :] = block[device * rows : (device + 1) * rows]
+
+    @pl.when(jnp.logical_not(swapped))
+    def _():
+        frequency = iota((extent, box_side), 0)
+        store(
+            matmul_split(table, operand(0)),
+            jnp.minimum(frequency, extent - frequency),
+        )
+
+    @pl.when(swapped)
+    def _():
+        store(matmul_split(table, operand(1), ((1,), (1,))), None)
+
+    lane = iota((devices, LANES), 1)
+    slot = half * NCLASS + jnp.where(swapped, wedge + 1, 0)
+    labels = jnp.where(lane == slot, 1.0, 0.0) + jnp.where(lane == slot + NSLOT, second, 0.0)
+    place = lane - ROW_LANE
+    frequency = iota((devices, LANES), 0) * rows + (place & (rows - 1))
+    block = place // rows
+    kept_plane = jnp.abs(block % planes - planes // 2) * (extent // planes)
+    kept = kept_plane * run <= jnp.minimum(frequency, extent - frequency) * rise
+    ours = (block // planes == half) & (place >= 0) & jnp.logical_not(swapped)
+    labels = labels + jnp.where(kept & ours, 1.0, 0.0)
+    out_ref[pl.ds(stride - 1, devices, stride=stride), :] = labels
+
+
+def average_kernel(rows, planes, arrived_ref, shell_ref, high_ref, low_ref, out_ref):
+    extent = shell_ref.shape[2]
+    devices = extent // rows
+    stride = arrived_ref.shape[0] // devices
+    out_stride = out_ref.shape[0] // devices
+    plane_abs = [abs(plane - planes // 2) * (extent // planes) for plane in range(planes)]
+    labels = arrived_ref[pl.ds(stride - 1, devices, stride=stride), :]
+    labels_low = labels.astype(jnp.bfloat16)
+
+    slot_rows = 2 * NSLOT * rows
+    slot_of = jnp.where(
+        iota((slot_rows, LANES), 0) // rows == iota((slot_rows, LANES), 1), 1.0, 0.0
+    ).astype(jnp.bfloat16)
+    by_particle = matmul(slot_of, labels_low, ((1,), (1,))).astype(jnp.bfloat16)
+    spread = jnp.where(
+        iota((devices, extent), 1) // rows == iota((devices, extent), 0), 1.0, 0.0
+    ).astype(jnp.bfloat16)
+    chosen = matmul(by_particle, spread)
+    same_row = (iota((slot_rows, extent), 0) & (rows - 1)) == (
+        iota((slot_rows, extent), 1) & (rows - 1)
+    )
+    chosen = jnp.where(same_row, chosen, 0.0).astype(jnp.bfloat16)
+    columns = []
+    for block in range(2 * planes):
+        pieces = [
+            arrived_ref[device * stride + block * rows : device * stride + (block + 1) * rows, :]
+            for device in range(devices)
+        ]
+        columns.append(jnp.concatenate(pieces, axis=0))
+    stacked = split(jnp.concatenate(columns, axis=1))
+    sums = matmul(chosen, stacked[1]) + matmul(chosen, stacked[0])
+
+    class_rows = NSLOT * rows
+    left = []
+    for part in range(2):
+        for plane in range(planes):
+            plain = sums[:class_rows, (part * planes + plane) * LANES :][:, :LANES]
+            other = sums[class_rows:, ((1 - part) * planes + plane) * LANES :][:, :LANES]
+            left.append(jnp.concatenate([plain, other if part == 0 else -other], axis=1))
+    lower = extent - LANES // 2
+    forward = [
+        jnp.concatenate(
+            [ref[lower:, :extent], ref[: LANES // 2, :extent]]
+            + [ref[lower:, extent:], ref[: LANES // 2, extent:]],
+            axis=0,
+        )
+        for ref in (high_ref, low_ref)
+    ]
+    turned = matmul_split(split(jnp.concatenate(left, axis=0)), forward)
+
+    counts = matmul(jnp.ones((rows, devices), jnp.bfloat16), labels_low)
+    lane = iota((rows, LANES), 1)
+    frequency = iota((1, extent), 1)
+    frequency_abs = jnp.minimum(frequency, extent - frequency)
+    masks = [
+        [
+            None
+            if plane_abs[plane] == 0
+            else plane_abs[plane] * wedge_run[wedge] <= frequency_abs * wedge_rise[wedge]
+            for wedge in range(NWEDGE)
+        ]
+        for plane in range(planes)
+    ]
+    averages = {}
+    for half in range(2):
+        swapped_counts = [
+            jnp.sum(
+                jnp.where(lane == half * NCLASS + 1 + wedge, counts, 0.0), axis=1, keepdims=True
+            )
+            for wedge in range(NWEDGE)
+        ]
+        for plane in range(planes):
+            place = ROW_LANE + (half * planes + plane) * rows
+            cover = jnp.sum(
+                jnp.where(lane == place + iota((rows, LANES), 0), counts, 0.0),
+                axis=1,
+                keepdims=True,
+            )
+            cover = jnp.broadcast_to(cover, (rows, extent))
+            for wedge in range(NWEDGE):
+                mask = masks[plane][wedge]
+                if mask is None:
+                    cover = cover + swapped_counts[wedge]
+                else:
+                    cover = cover + jnp.where(mask, swapped_counts[wedge], 0.0)
+            inverse = 1.0 / jnp.maximum(cover, 1.0)
+            for part in range(2):
+                base = ((part * planes + plane) * NSLOT + half * NCLASS) * rows
+                total = turned[base : base + rows]
+                for wedge in range(NWEDGE):
+                    start = base + (1 + wedge) * rows
+                    term = turned[start : start + rows]
+                    mask = masks[plane][wedge]
+                    total = total + (term if mask is None else jnp.where(mask, term, 0.0))
+                averages[half, part, plane] = total * inverse
+
+    shell_index = iota((NSHELL, extent), 0)
+    accumulated = [jnp.zeros((NSHELL, extent), jnp.float32) for _ in range(3)]
+    for plane in range(planes):
+        a_re, a_im = averages[0, 0, plane], averages[0, 1, plane]
+        b_re, b_im = averages[1, 0, plane], averages[1, 1, plane]
+        products = (
+            a_re * b_re + a_im * b_im,
+            a_re * a_re + a_im * a_im,
+            b_re * b_re + b_im * b_im,
+        )
+        shells = shell_ref[plane]
+        for row in range(rows):
+            member = shells[row : row + 1] == shell_index
+            for which in range(3):
+                accumulated[which] = accumulated[which] + jnp.where(
+                    member, products[which][row : row + 1], 0.0
+                )
+    accumulated.append(jnp.zeros((LANES - 3 * NSHELL, extent), jnp.float32))
+    gathered = jnp.concatenate(accumulated, axis=0)
+    pieces = []
+    for _ in range(3):
+        piece = gathered.astype(jnp.bfloat16)
+        gathered = gathered - piece.astype(jnp.float32)
+        pieces.append(piece)
+    shell_sums = matmul(
+        jnp.ones((SUBLANES, 3 * extent), jnp.bfloat16),
+        jnp.concatenate(pieces, axis=1),
+        ((1,), (1,)),
+    )
+    out_ref[pl.ds(out_stride - 1, devices, stride=out_stride), :] = jnp.broadcast_to(
+        shell_sums[:1], (devices, LANES)
+    )
+
+    order = [(half, plane) for half in range(2) for plane in range(planes)]
+    backward = jnp.concatenate(
+        [averages[half, part, plane] for part in range(2) for half, plane in order], axis=0
+    )
+    back = matmul_split(split(backward), [high_ref[...], low_ref[...]])
+    offset = len(order) * rows
+    blocks = {}
+    for number, (half, plane) in enumerate(order):
+        real = back[number * rows : (number + 1) * rows]
+        imag = back[offset + number * rows : offset + (number + 1) * rows]
+        blocks[half, 0, plane] = real[:, :extent] - imag[:, extent:]
+        blocks[half, 1, plane] = real[:, extent:] + imag[:, :extent]
+    sequence = [
+        blocks[half, part, plane]
+        for half in range(2)
+        for part in range(2)
+        for plane in range(planes)
+    ]
+    lane = iota((rows, LANES), 1)
+    straight = lane // (LANES // 2) == iota((rows, LANES), 0) // (rows // 2)
+    group_size = LANES // rows
+    for group in range(extent // LANES):
+        tiles = [block[:, group * LANES : (group + 1) * LANES] for block in sequence]
+        distance = 1
+        while distance < len(tiles):
+            shift = distance * rows
+            clear = (lane & shift) == 0
+            for low in range(len(tiles)):
+                if low & distance:
+                    continue
+                high = low | distance
+                a, b = tiles[low], tiles[high]
+                tiles[low] = jnp.where(clear, a, pltpu.roll(b, shift, 1))
+                tiles[high] = jnp.where(clear, pltpu.roll(a, LANES - shift, 1), b)
+            distance *= 2
+        for number, tile in enumerate(tiles):
+            crossed = pltpu.roll(pltpu.roll(tile, LANES // 2, 1), rows // 2, 0)
+            packed = jnp.where(straight, tile, crossed)
+            for upper in range(2):
+                device = group * group_size + upper * (group_size // 2) + number
+                start = device * out_stride
+                out_ref[start : start + rows // 2, :] = packed[
+                    upper * (rows // 2) : (upper + 1) * (rows // 2)
+                ]
+
+
+def finish_kernel(rows, arrived_ref, high_ref, low_ref, maps_ref, fsc_ref):
+    halves, parts, planes, own, extent = maps_ref.shape
+    devices = extent // rows
+    stride = arrived_ref.shape[0] // devices
+    total = jnp.sum(
+        arrived_ref[pl.ds(stride - 1, devices, stride=stride), :], axis=0, keepdims=True
+    )
+    cross = total[:, :NSHELL]
+    power = total[:, NSHELL : 2 * NSHELL] * total[:, 2 * NSHELL : 3 * NSHELL]
+    fsc_ref[...] = cross / (jnp.sqrt(power) + 1e-06)
+
+    gathered = jnp.concatenate(
+        [arrived_ref[pl.ds(row, devices, stride=stride), :] for row in range(rows // 2)], axis=0
+    )
+    turned = gathered.T
+    left = jnp.concatenate([turned[: LANES // 2], turned[LANES // 2 :]], axis=1)
+    final = matmul_split(split(left), [high_ref[...], low_ref[...]])
+    for half in range(halves):
+        for plane in range(planes):
+            real_at = ((half * parts + 0) * planes + plane) * own
+            imag_at = ((half * parts + 1) * planes + plane) * own
+            real = final[real_at : real_at + own]
+            imag = final[imag_at : imag_at + own]
+            maps_ref[half, 0, plane] = real[:, :extent] - imag[:, extent:]
+            maps_ref[half, 1, plane] = real[:, extent:] + imag[:, :extent]
+
+
+def in_vmem(count):
+    return [pl.BlockSpec(memory_space=pltpu.VMEM)] * count
+
+
+def exchange(values, devices):
+    chunks = values.reshape(devices, values.shape[0] // devices, 1, LANES)
+    return lax.all_to_all(chunks, axes, 0, 0, tiled=True).reshape(values.shape)
+
+
+def fits(particles, shell_map, devices):
+    rows = shell_map.shape[1]
+    planes = particles.shape[2]
+    extent = shell_map.shape[2]
+    return (
+        particles.shape[0] == 1
+        and rows == SUBLANES
+        and rows * devices == extent
+        and particles.shape[3] == LANES
+        and extent % LANES == 0
+        and 4 * planes * rows * 2 == LANES
+        and ROW_LANE + 2 * planes * rows <= LANES
+        and extent * 2 >= LANES
+    )
+
+
+def shards(particles, orientation, wedge_index, half_set, shell_map):
+    devices = lax.axis_size("px") * lax.axis_size("py")
+    if not fits(particles, shell_map, devices):
+        return general(particles, orientation, wedge_index, half_set, shell_map)
+    planes = particles.shape[2]
+    box_side = particles.shape[3]
+    rows = shell_map.shape[1]
+    extent = shell_map.shape[2]
+    spectral = np.arange(extent)
+    smem = [pl.BlockSpec(memory_space=pltpu.SMEM)] * 3
+
+    along_x = np.concatenate(
+        cos_sin(spectral, np.arange(box_side) - box_side // 2, extent), axis=1
+    )
+    x_high, x_low = split_table(along_x)
+    full = np.concatenate(cos_sin(spectral, spectral, extent), axis=1)
+    y_high, y_low = split_table(full)
+    half_rows = rows // 2
+    arrival = (
+        np.arange(2)[:, None, None] * half_rows
+        + np.arange(half_rows)[None, :, None]
+        + np.arange(devices)[None, None, :] * rows
+    ).reshape(-1)
+    back_high, back_low = split_table(full[arrival])
+
+    sent = pl.pallas_call(
+        functools.partial(spread_kernel, rows),
+        out_shape=jax.ShapeDtypeStruct((devices * (2 * planes * rows + 1), LANES), jnp.float32),
+        in_specs=smem + in_vmem(3),
+        out_specs=in_vmem(1)[0],
+    )(orientation, wedge_index, half_set, particles, x_high, x_low)
+    arrived = exchange(sent, devices)
+    middle = pl.pallas_call(
+        functools.partial(average_kernel, rows, planes),
+        out_shape=jax.ShapeDtypeStruct((devices * (half_rows + 1), LANES), jnp.float32),
+        in_specs=in_vmem(4),
+        out_specs=in_vmem(1)[0],
+    )(arrived, shell_map, y_high, y_low)
+    returned = exchange(middle, devices)
+    half_maps, fsc = pl.pallas_call(
+        functools.partial(finish_kernel, rows),
+        out_shape=(
+            jax.ShapeDtypeStruct((2, 2, planes, rows, extent), jnp.float32),
+            jax.ShapeDtypeStruct((1, NSHELL), jnp.float32),
+        ),
+        in_specs=in_vmem(3),
+        out_specs=tuple(in_vmem(2)),
+    )(returned, back_high, back_low)
+    return half_maps, fsc.reshape(NSHELL)
 
 
 def select(lookup, position):
@@ -35,7 +439,7 @@
     )
 
 
-def shards(particles, orientation, wedge_index, half_set, shell_map):
+def general(particles, orientation, wedge_index, half_set, shell_map):
     planes = particles.shape[2]
     box_side = particles.shape[3]
     extent = shell_map.shape[2]

time: 241 us -> 44.9 us (0.19)
  waiting for transfers between devices: 93.5 us -> 0 us
  blocking collectives: 81.8 us -> 34.2 us
  other arithmetic: 18 us -> 0 us
  between operations: 16.4 us -> 2.57 us
  matrix products: 12.8 us -> 0 us
  local copies, waits for them, and re-layouts: 10.6 us -> 0 us
  Pallas kernels: 0 us -> 7.82 us
  starting transfers between devices: 6.93 us -> 0 us
    reduce_scatter x1 -> x0, waiting for transfers between devices: 89.9 us -> none  [shards(): lax.psum_scatter(totals, ('px', 'py'), scatter_dimension=3, tiled=True)]
    psum x2 -> x0, blocking collectives: 81.8 us -> none  [the longest x1 42 us: shards(): class_totals = lax.psum(local_counts, ('px', 'py'))]
    all_to_all x0 -> x2, blocking collectives: none -> 34.2 us  [exchange(): return lax.all_to_all(chunks, axes, 0, 0, tiled=True).reshape(values.shape)]
    dot_general x11 -> x0, matrix products: 12.8 us -> none  [the longest x1 2.02 us: shards(): along_sin = jnp.einsum('czab,bk->czak', source, sin_fwd, precision=highest)]
    mul x12 -> x0, other arithmetic: 9.22 us -> none  [the longest x7 6 us: coverage(): spectral_abs[None, :] * rise_value]
    pallas_call x0 -> x3, Pallas kernels: none -> 7.82 us  [the longest x1 3.52 us: shards(): pl.pallas_call(functools.partial(average_kernel, rows, planes), out_shape...]
    unnamed x22 -> x0, local copies, waits for them, and re-layouts: 7.03 us -> none
    all_to_all x2 -> x0, starting transfers between devices: 6.89 us -> none  [the longest x1 3.54 us: shards(): lax.all_to_all(lax.all_to_all(middle, 'px', split_axis=3, concat_axis=4,...]
  transfers between devices with their start and end apart: 3 -> 0, of which waited for: 2 -> 0; matrix products, arithmetic and copies ran while one was open for 4% -> 0% of each run, Pallas kernels for 0% -> 0%
where the time goes in v1:
time: 44.9 us; the launch traced here: 44.6 us
  blocking collectives  34.2 us (76%)
  Pallas kernels  7.82 us (17%)
  between operations  2.57 us (6%)
    all_to_all x2, blocking collectives, exchange(): return lax.all_to_all(chunks, axes, 0, 0, tiled=True).reshape(values.shape)  34.2 us
    pallas_call x1, Pallas kernels, shards(): pl.pallas_call(functools.partial(average_kernel, rows, planes), out_shape...  3.52 us
    pallas_call x1, Pallas kernels, shards(): pl.pallas_call(functools.partial(spread_kernel, rows), out_shape=jax.Shap...  2.28 us
    pallas_call x1, Pallas kernels, shards(): pl.pallas_call(functools.partial(finish_kernel, rows), out_shape=(jax.Sha...  2.02 us

profile of v1, /device:TPU:0, one launch (start us, length us, event | category | flops | bytes accessed | tf_op | source)
XLA Modules:
  0.0 44.6 jit_solution(5794422352148688894)
XLA Ops:
  2.6 2.3 %shard_map.122 = f32[1056,128]{1,0:T(8,128)} custom-call(s32[1]{0:T(128)S(6)} %copy.15.turn_ref, s32[1]{0:T(128)S(6)} %copy.16.wedge_ref, s32[1]{0:T(128)S(6)} %copy.17.half_ref, f32[1,2,2,128,128]{4,3,2,1,0:T(8,128)} %source_ref.1, bf16[256,256]{1,0:T(8,128)(2,1)} %constant.12.clone.high_ref, bf16[256,256]{1,0:T(8,128)(2,1)} %constant.13.clone.low_ref), custom_call_target="tpu_custom_call" | custom-call | tf_op jit(solution)/shard_map/pallas_call | solution.py:396
  4.8 23.4 %all_to_all.10 = f32[32,33,1,128]{3,2,1,0:T(1,128)} all-to-all(f32[32,33,1,128]{3,2,1,0:T(1,128)} %bitcast.5), channel_id=1, replica_groups=mesh['px'=8,'py'=4] {'px','py'}, dimensions={0} | all-to-all | bytes 1081344 | tf_op jit(solution)/shard_map/all_to_all | solution.py:352
  28.2 3.5 %shard_map.123 = f32[160,128]{1,0:T(8,128)} custom-call(f32[1056,128]{1,0:T(8,128)} %bitcast.6, s32[2,8,256]{2,1,0:T(8,128)} %shell_ref.1, bf16[256,512]{1,0:T(8,128)(2,1)} %constant.14.clone.high_ref, bf16[256,512]{1,0:T(8,128)(2,1)} %constant.15.clone.low_ref), custom_call_target="tpu_custom_call" | custom-call | tf_op jit(solution)/shard_map/pallas_call | solution.py:403
  31.7 10.8 %all_to_all.11 = f32[32,5,1,128]{3,2,1,0:T(1,128)} all-to-all(f32[32,5,1,128]{3,2,1,0:T(1,128)} %bitcast.7), channel_id=1, replica_groups=mesh['px'=8,'py'=4] {'px','py'}, dimensions={0} | all-to-all | bytes 163840 | tf_op jit(solution)/shard_map/all_to_all | solution.py:352
  42.6 2.0 %shard_map.124 = (f32[2,2,2,8,256]{4,3,2,1,0:T(8,128)}, f32[1,32]{1,0:T(1,128)}) custom-call(f32[160,128]{1,0:T(8,128)} %bitcast.8, bf16[256,512]{1,0:T(8,128)(2,1)} %constant.16.clone.high_ref, bf16[256,512]{1,0:T(8,128)(2,1)} %constant.17.clone.low_ref), custom_call_target="tpu_custom_call" | custom-call | tf_op jit(solution)/shard_map/pallas_call | solution.py:410

commit v2 on v1

--- a/solution.py
+++ b/solution.py
@@ -69,7 +69,23 @@
     return lax.broadcasted_iota(jnp.int32, shape, dimension)
 
 
-def spread_kernel(rows, turn_ref, wedge_ref, half_ref, source_ref, high_ref, low_ref, out_ref):
+def spread_kernel(
+    rows, turn_ref, wedge_ref, half_ref, source_hbm, high_hbm, low_hbm, out_ref, *scratch
+):
+    source_ref, high_ref, low_ref, arrivals = scratch
+    pairs = (
+        (source_hbm, source_ref),
+        (high_hbm, high_ref),
+        (low_hbm, low_ref),
+    )
+    copies = [
+        pltpu.make_async_copy(there, here, arrivals.at[number])
+        for number, (there, here) in enumerate(pairs)
+    ]
+    for copy in copies:
+        copy.start()
+    for copy in copies:
+        copy.wait()
     planes = source_ref.shape[2]
     box_side = source_ref.shape[3]
     extent = high_ref.shape[0]
@@ -343,6 +359,9 @@
             maps_ref[half, 1, plane] = real[:, extent:] + imag[:, :extent]
 
 
+small_grant = pltpu.CompilerParams(vmem_limit_bytes=16 * 1024 * 1024)
+
+
 def in_vmem(count):
     return [pl.BlockSpec(memory_space=pltpu.VMEM)] * count
 
@@ -377,7 +396,6 @@
     rows = shell_map.shape[1]
     extent = shell_map.shape[2]
     spectral = np.arange(extent)
-    smem = [pl.BlockSpec(memory_space=pltpu.SMEM)] * 3
 
     along_x = np.concatenate(
         cos_sin(spectral, np.arange(box_side) - box_side // 2, extent), axis=1
@@ -396,15 +414,24 @@
     sent = pl.pallas_call(
         functools.partial(spread_kernel, rows),
         out_shape=jax.ShapeDtypeStruct((devices * (2 * planes * rows + 1), LANES), jnp.float32),
-        in_specs=smem + in_vmem(3),
+        in_specs=[pl.BlockSpec(memory_space=pltpu.SMEM)] * 3
+        + [pl.BlockSpec(memory_space=pltpu.HBM)] * 3,
         out_specs=in_vmem(1)[0],
-    )(orientation, wedge_index, half_set, particles, x_high, x_low)
+        scratch_shapes=[
+            pltpu.VMEM(particles.shape, jnp.float32),
+            pltpu.VMEM(x_high.shape, jnp.bfloat16),
+            pltpu.VMEM(x_low.shape, jnp.bfloat16),
+            pltpu.SemaphoreType.DMA((3,)),
+        ],
+        compiler_params=small_grant,
+    )(orientation, wedge_index, half_set, pltpu.with_memory_space_constraint(particles, pltpu.HBM), pltpu.with_memory_space_constraint(jnp.asarray(x_high), pltpu.HBM), pltpu.with_memory_space_constraint(jnp.asarray(x_low), pltpu.HBM))
     arrived = exchange(sent, devices)
     middle = pl.pallas_call(
         functools.partial(average_kernel, rows, planes),
         out_shape=jax.ShapeDtypeStruct((devices * (half_rows + 1), LANES), jnp.float32),
         in_specs=in_vmem(4),
         out_specs=in_vmem(1)[0],
+        compiler_params=small_grant,
     )(arrived, shell_map, y_high, y_low)
     returned = exchange(middle, devices)
     half_maps, fsc = pl.pallas_call(
@@ -415,6 +442,7 @@
         ),
         in_specs=in_vmem(3),
         out_specs=tuple(in_vmem(2)),
+        compiler_params=small_grant,
     )(returned, back_high, back_low)
     return half_maps, fsc.reshape(NSHELL)
 

time: 44.9 us -> 40.5 us (0.902)
  Pallas kernels: 7.82 us -> 4.16 us
  blocking collectives: 34.2 us -> 33.5 us
    pallas_call x1, Pallas kernels: 3.52 us -> 1.68 us  [shards(): pl.pallas_call(functools.partial(average_kernel, rows, planes), out_shape...]
    pallas_call x1, Pallas kernels: 2.02 us -> 0.95 us  [shards(): pl.pallas_call(functools.partial(finish_kernel, rows), out_shape=(jax.Sha...]
    all_to_all x2, blocking collectives: 34.2 us -> 33.5 us  [exchange(): return lax.all_to_all(chunks, axes, 0, 0, tiled=True).reshape(values.shape)]
    pallas_call x1, Pallas kernels: 2.28 us -> 1.53 us  [shards(): pl.pallas_call(functools.partial(spread_kernel, rows), out_shape=jax.Shap...]
where the time goes in v2:
time: 40.5 us; the launch traced here: 40.3 us
  blocking collectives  33.5 us (83%)
  Pallas kernels  4.16 us (10%)
  between operations  2.63 us (6%)
    all_to_all x2, blocking collectives, exchange(): return lax.all_to_all(chunks, axes, 0, 0, tiled=True).reshape(values.shape)  33.5 us
    pallas_call x1, Pallas kernels, shards(): pl.pallas_call(functools.partial(average_kernel, rows, planes), out_shape...  1.68 us
    pallas_call x1, Pallas kernels, shards(): pl.pallas_call(functools.partial(spread_kernel, rows), out_shape=jax.Shap...  1.53 us
    pallas_call x1, Pallas kernels, shards(): pl.pallas_call(functools.partial(finish_kernel, rows), out_shape=(jax.Sha...  0.95 us

profile of v2, /device:TPU:0, one launch (start us, length us, event | category | flops | bytes accessed | tf_op | source)
XLA Modules:
  0.0 40.3 jit_solution(6030197621416674134)
XLA Ops:
  2.6 1.5 %shard_map.122 = f32[1056,128]{1,0:T(8,128)S(1)} custom-call(s32[1]{0:T(128)S(6)} %copy.15.turn_ref, s32[1]{0:T(128)S(6)} %copy.16.wedge_ref, s32[1]{0:T(128)S(6)} %copy.17.half_ref, f32[1,2,2,128,128]{4,3,2,1,0:T(8,128)} %source_hbm.1, bf16[256,256]{1,0:T(8,128)(2,1)} %constant.12.clone.high_hbm, bf16[256,256]{1,0:T(8,128)(2,1)} %constant.13.clone.low_hbm), custom_call_target="tpu_custom_call" | custom-call | tf_op jit(solution)/shard_map/pallas_call | solution.py:414
  4.1 0.0 copy-start.2
  4.1 0.0 copy-start.3
  4.1 0.0 copy-start.4
  4.1 23.0 %all_to_all.10 = f32[32,33,1,128]{3,2,1,0:T(1,128)S(1)} all-to-all(f32[32,33,1,128]{3,2,1,0:T(1,128)S(1)} %bitcast.5), channel_id=1, replica_groups=mesh['px'=8,'py'=4] {'px','py'}, dimensions={0} | all-to-all | bytes 1081344 | tf_op jit(solution)/shard_map/all_to_all | solution.py:371
  27.2 0.0 copy-done.2
  27.2 0.0 copy-done.3
  27.2 0.0 copy-done.4
  27.2 0.0 copy-start
  27.2 0.0 copy-start.1
  27.2 1.7 %shard_map.123 = f32[160,128]{1,0:T(8,128)S(1)} custom-call(f32[1056,128]{1,0:T(8,128)S(1)} %bitcast.6, s32[2,8,256]{2,1,0:T(8,128)S(1)} %copy-done.4, bf16[256,512]{1,0:T(8,128)(2,1)S(1)} %copy-done.3, bf16[256,512]{1,0:T(8,128)(2,1)S(1)} %copy-done.2), custom_call_target="tpu_custom_call" | custom-call | tf_op jit(solution)/shard_map/pallas_call | solution.py:429
  28.9 10.4 %all_to_all.11 = f32[32,5,1,128]{3,2,1,0:T(1,128)S(1)} all-to-all(f32[32,5,1,128]{3,2,1,0:T(1,128)S(1)} %bitcast.7), channel_id=1, replica_groups=mesh['px'=8,'py'=4] {'px','py'}, dimensions={0} | all-to-all | bytes 163840 | tf_op jit(solution)/shard_map/all_to_all | solution.py:371
  39.3 0.0 copy-done
  39.3 0.0 copy-done.1
  39.3 1.0 %shard_map.124 = (f32[2,2,2,8,256]{4,3,2,1,0:T(8,128)}, f32[1,32]{1,0:T(1,128)}) custom-call(f32[160,128]{1,0:T(8,128)S(1)} %bitcast.8, bf16[256,512]{1,0:T(8,128)(2,1)S(1)} %copy-done.1, bf16[256,512]{1,0:T(8,128)(2,1)S(1)} %copy-done), custom_call_target="tpu_custom_call" | custom-call | tf_op jit(solution)/shard_map/pallas_call | solution.py:437
Async XLA Ops:
  4.1 23.1 %copy-start.2 = (bf16[256,512]{1,0:T(8,128)(2,1)S(1)}, bf16[256,512]{1,0:T(8,128)(2,1)}, u32[]{:S(2)}) copy-start(bf16[256,512]{1,0:T(8,128)(2,1)} %constant.15.clone.low_ref) | copy-start | bytes 786436
  4.1 23.1 %copy-start.3 = (bf16[256,512]{1,0:T(8,128)(2,1)S(1)}, bf16[256,512]{1,0:T(8,128)(2,1)}, u32[]{:S(2)}) copy-start(bf16[256,512]{1,0:T(8,128)(2,1)} %constant.14.clone.high_ref) | copy-start | bytes 786436
  4.1 23.1 %copy-start.4 = (s32[2,8,256]{2,1,0:T(8,128)S(1)}, s32[2,8,256]{2,1,0:T(8,128)}, u32[]{:S(2)}) copy-start(s32[2,8,256]{2,1,0:T(8,128)} %shell_ref.1) | copy-start | bytes 49156
  27.2 12.1 %copy-start = (bf16[256,512]{1,0:T(8,128)(2,1)S(1)}, bf16[256,512]{1,0:T(8,128)(2,1)}, u32[]{:S(2)}) copy-start(bf16[256,512]{1,0:T(8,128)(2,1)} %constant.17.clone.low_ref) | copy-start | bytes 786436
  27.2 12.1 %copy-start.1 = (bf16[256,512]{1,0:T(8,128)(2,1)S(1)}, bf16[256,512]{1,0:T(8,128)(2,1)}, u32[]{:S(2)}) copy-start(bf16[256,512]{1,0:T(8,128)(2,1)} %constant.16.clone.high_ref) | copy-start | bytes 786436

commit v3 on v1

--- a/solution.py
+++ b/solution.py
@@ -24,6 +24,7 @@
 NWEDGE = len(wedge_rise)
 NCLASS = 1 + NWEDGE
 NSLOT = 2 * NCLASS
+HALF_LANE = 2 * NSLOT
 ROW_LANE = 32
 
 
@@ -58,6 +59,12 @@
     )
 
 
+def matmul_rows(left, right):
+    count = left[0].shape[0]
+    both = matmul(jnp.concatenate(left, axis=0), right[0])
+    return both[:count] + (both[count:] + matmul(left[0], right[1]))
+
+
 def pick(lookup, position):
     value = jnp.int32(lookup[0])
     for entry in range(1, len(lookup)):
@@ -69,26 +76,50 @@
     return lax.broadcasted_iota(jnp.int32, shape, dimension)
 
 
-def spread_kernel(rows, turn_ref, wedge_ref, half_ref, source_ref, high_ref, low_ref, out_ref):
+def label_kernel(rows, planes, extent, turn_ref, wedge_ref, half_ref, label_ref):
+    devices = extent // rows
+    turn = turn_ref[0]
+    wedge = wedge_ref[0]
+    half = half_ref[0]
+    swapped = (turn & 1) == 1
+    second = jnp.where(((turn + 2) & 4) == 4, -1.0, 1.0)
+    rise = pick(wedge_rise, wedge)
+    run = pick(wedge_run, wedge)
+    lane = iota((devices, LANES), 1)
+    slot = half * NCLASS + jnp.where(swapped, wedge + 1, 0)
+    ones = (lane == slot) | (lane == HALF_LANE + half)
+    signs = (lane == NSLOT + slot) | (lane == HALF_LANE + 2 + half)
+    labels = jnp.where(ones, 1.0, jnp.where(signs, second, 0.0))
+    place = lane - ROW_LANE
+    frequency = iota((devices, LANES), 0) * rows + (place & (rows - 1))
+    block = place // rows
+    kept_plane = jnp.abs(block % planes - planes // 2) * (extent // planes)
+    kept = kept_plane * run <= jnp.minimum(frequency, extent - frequency) * rise
+    ours = (block // planes == half) & (place >= 0) & jnp.logical_not(swapped)
+    labels = labels + jnp.where(kept & ours, 1.0, 0.0)
+    label_ref[...] = labels
+
+
+def spread_kernel(rows, turn_ref, wedge_ref, source_ref, table_ref, label_ref, out_ref):
     planes = source_ref.shape[2]
     box_side = source_ref.shape[3]
-    extent = high_ref.shape[0]
+    extent = table_ref.shape[0]
     devices = extent // rows
     stride = out_ref.shape[0] // devices
     turn = turn_ref[0]
     wedge = wedge_ref[0]
-    half = half_ref[0]
     swapped = (turn & 1) == 1
     first = jnp.where(((turn + 1) & 2) == 2, -1.0, 1.0)
-    second = jnp.where(((turn + 2) & 4) == 4, -1.0, 1.0)
     rise = pick(wedge_rise, wedge)
     run = pick(wedge_run, wedge)
     plane_abs = [abs(plane - planes // 2) * (extent // planes) for plane in range(planes)]
 
     sign = jnp.full((1, box_side), first, jnp.float32).astype(jnp.bfloat16)
     table = []
-    for ref in (high_ref, low_ref):
-        table.append(jnp.concatenate([ref[:, :box_side], ref[:, box_side:] * sign], axis=1))
+    for start in (0, 2 * box_side):
+        cosine = table_ref[:, start : start + box_side]
+        sine = table_ref[:, start + box_side : start + 2 * box_side]
+        table.append(jnp.concatenate([cosine, sine * sign], axis=1))
 
     def operand(axis):
         parts = ([], [])
@@ -128,21 +159,45 @@
     def _():
         store(matmul_split(table, operand(1), ((1,), (1,))), None)
 
-    lane = iota((devices, LANES), 1)
-    slot = half * NCLASS + jnp.where(swapped, wedge + 1, 0)
-    labels = jnp.where(lane == slot, 1.0, 0.0) + jnp.where(lane == slot + NSLOT, second, 0.0)
-    place = lane - ROW_LANE
-    frequency = iota((devices, LANES), 0) * rows + (place & (rows - 1))
-    block = place // rows
-    kept_plane = jnp.abs(block % planes - planes // 2) * (extent // planes)
-    kept = kept_plane * run <= jnp.minimum(frequency, extent - frequency) * rise
-    ours = (block // planes == half) & (place >= 0) & jnp.logical_not(swapped)
-    labels = labels + jnp.where(kept & ours, 1.0, 0.0)
-    out_ref[pl.ds(stride - 1, devices, stride=stride), :] = labels
-
-
-def average_kernel(rows, planes, arrived_ref, shell_ref, high_ref, low_ref, out_ref):
-    extent = shell_ref.shape[2]
+    out_ref[pl.ds(stride - 1, devices, stride=stride), :] = label_ref[...]
+
+
+def fill_flags(rows, shell_ref, member_ref, spread_ref, block_ref):
+    planes, _, extent = shell_ref.shape
+    shell_index = iota((NSHELL, extent), 0)
+    for plane in range(planes):
+        shells = shell_ref[plane]
+        for row in range(rows):
+            start = (plane * rows + row) * NSHELL
+            member = shells[row : row + 1] == shell_index
+            member_ref[start : start + NSHELL, :] = jnp.where(member, 1.0, 0.0).astype(
+                jnp.bfloat16
+            )
+
+    def flag(ref, condition):
+        ref[...] = jnp.where(condition, 1.0, 0.0).astype(ref.dtype)
+
+    flag(spread_ref, iota(spread_ref.shape, 1) // rows == iota(spread_ref.shape, 0))
+    flag(
+        block_ref,
+        iota(block_ref.shape, 0) % (planes * rows) == iota(block_ref.shape, 1) // NSHELL,
+    )
+
+
+def average_kernel(
+    rows,
+    planes,
+    arrived_ref,
+    shell_ref,
+    high_ref,
+    low_ref,
+    out_ref,
+    member_ref,
+    spread_ref,
+    block_ref,
+):
+    extent = high_ref.shape[0]
+    fill_flags(rows, shell_ref, member_ref, spread_ref, block_ref)
     devices = extent // rows
     stride = arrived_ref.shape[0] // devices
     out_stride = out_ref.shape[0] // devices
@@ -150,36 +205,37 @@
     labels = arrived_ref[pl.ds(stride - 1, devices, stride=stride), :]
     labels_low = labels.astype(jnp.bfloat16)
 
-    slot_rows = 2 * NSLOT * rows
-    slot_of = jnp.where(
-        iota((slot_rows, LANES), 0) // rows == iota((slot_rows, LANES), 1), 1.0, 0.0
+    slots = HALF_LANE + 4
+    by_slot = matmul(labels.T[:ROW_LANE].astype(jnp.bfloat16), spread_ref[...])
+    same_row = iota((rows, extent), 0) == (iota((rows, extent), 1) & (rows - 1))
+    chosen = jnp.concatenate(
+        [jnp.where(same_row, by_slot[slot : slot + 1], 0.0) for slot in range(slots)], axis=0
     ).astype(jnp.bfloat16)
-    by_particle = matmul(slot_of, labels_low, ((1,), (1,))).astype(jnp.bfloat16)
-    spread = jnp.where(
-        iota((devices, extent), 1) // rows == iota((devices, extent), 0), 1.0, 0.0
-    ).astype(jnp.bfloat16)
-    chosen = matmul(by_particle, spread)
-    same_row = (iota((slot_rows, extent), 0) & (rows - 1)) == (
-        iota((slot_rows, extent), 1) & (rows - 1)
-    )
-    chosen = jnp.where(same_row, chosen, 0.0).astype(jnp.bfloat16)
-    columns = []
-    for block in range(2 * planes):
-        pieces = [
-            arrived_ref[device * stride + block * rows : device * stride + (block + 1) * rows, :]
-            for device in range(devices)
-        ]
-        columns.append(jnp.concatenate(pieces, axis=0))
-    stacked = split(jnp.concatenate(columns, axis=1))
-    sums = matmul(chosen, stacked[1]) + matmul(chosen, stacked[0])
-
-    class_rows = NSLOT * rows
     left = []
-    for part in range(2):
-        for plane in range(planes):
-            plain = sums[:class_rows, (part * planes + plane) * LANES :][:, :LANES]
-            other = sums[class_rows:, ((1 - part) * planes + plane) * LANES :][:, :LANES]
-            left.append(jnp.concatenate([plain, other if part == 0 else -other], axis=1))
+    base = {}
+    height = 0
+    for plane in range(planes):
+        columns = []
+        for part in range(2):
+            block = part * planes + plane
+            pieces = [
+                arrived_ref[device * stride + block * rows : device * stride + (block + 1) * rows]
+                for device in range(devices)
+            ]
+            columns.append(jnp.concatenate(pieces, axis=0))
+        stacked = split(jnp.concatenate(columns, axis=1))
+        if plane_abs[plane] == 0:
+            own = chosen[HALF_LANE * rows : (HALF_LANE + 4) * rows]
+        else:
+            own = chosen[: 2 * NSLOT * rows]
+        sums = matmul(own, stacked[1]) + matmul(own, stacked[0])
+        count = own.shape[0] // 2
+        plain, signed = sums[:count], sums[count:]
+        left.append(jnp.concatenate([plain[:, :LANES], signed[:, LANES:]], axis=1))
+        left.append(jnp.concatenate([plain[:, LANES:], -signed[:, :LANES]], axis=1))
+        base[0, plane] = height
+        base[1, plane] = height + count
+        height += 2 * count
     lower = extent - LANES // 2
     forward = [
         jnp.concatenate(
@@ -189,7 +245,7 @@
         )
         for ref in (high_ref, low_ref)
     ]
-    turned = matmul_split(split(jnp.concatenate(left, axis=0)), forward)
+    turned = matmul_rows(split(jnp.concatenate(left, axis=0)), forward)
 
     counts = matmul(jnp.ones((rows, devices), jnp.bfloat16), labels_low)
     lane = iota((rows, LANES), 1)
@@ -228,53 +284,55 @@
                     cover = cover + jnp.where(mask, swapped_counts[wedge], 0.0)
             inverse = 1.0 / jnp.maximum(cover, 1.0)
             for part in range(2):
-                base = ((part * planes + plane) * NSLOT + half * NCLASS) * rows
-                total = turned[base : base + rows]
-                for wedge in range(NWEDGE):
-                    start = base + (1 + wedge) * rows
-                    term = turned[start : start + rows]
-                    mask = masks[plane][wedge]
-                    total = total + (term if mask is None else jnp.where(mask, term, 0.0))
+                start = base[part, plane]
+                if plane_abs[plane] == 0:
+                    start += half * rows
+                    total = turned[start : start + rows]
+                else:
+                    start += half * NCLASS * rows
+                    total = turned[start : start + rows]
+                    for wedge in range(NWEDGE):
+                        start += rows
+                        term = turned[start : start + rows]
+                        total = total + jnp.where(masks[plane][wedge], term, 0.0)
                 averages[half, part, plane] = total * inverse
 
-    shell_index = iota((NSHELL, extent), 0)
-    accumulated = [jnp.zeros((NSHELL, extent), jnp.float32) for _ in range(3)]
+    order = [(half, plane) for half in range(2) for plane in range(planes)]
+    backward = jnp.concatenate(
+        [averages[half, part, plane] for part in range(2) for half, plane in order], axis=0
+    )
+    back = matmul_rows(split(backward), [high_ref[...], low_ref[...]])
+    products = ([], [], [])
     for plane in range(planes):
         a_re, a_im = averages[0, 0, plane], averages[0, 1, plane]
         b_re, b_im = averages[1, 0, plane], averages[1, 1, plane]
-        products = (
-            a_re * b_re + a_im * b_im,
-            a_re * a_re + a_im * a_im,
-            b_re * b_re + b_im * b_im,
+        products[0].append(a_re * b_re + a_im * b_im)
+        products[1].append(a_re * a_re + a_im * a_im)
+        products[2].append(b_re * b_re + b_im * b_im)
+    parts = split(jnp.concatenate(products[0] + products[1] + products[2], axis=0))
+    by_row = matmul(jnp.concatenate(parts, axis=0), member_ref[...], ((1,), (1,)))
+    count = by_row.shape[0] // 2
+    by_row = by_row[:count] + by_row[count:]
+    by_row = by_row * block_ref[...]
+    row_lane = iota((1, LANES), 1)
+    shell_sums = jnp.zeros((1, LANES), jnp.float32)
+    for which in range(3):
+        block = by_row[which * planes * rows : (which + 1) * planes * rows]
+        folded = sum(
+            block[plane * rows : (plane + 1) * rows, start : start + LANES]
+            for plane in range(planes)
+            for start in range(0, by_row.shape[1], LANES)
         )
-        shells = shell_ref[plane]
-        for row in range(rows):
-            member = shells[row : row + 1] == shell_index
-            for which in range(3):
-                accumulated[which] = accumulated[which] + jnp.where(
-                    member, products[which][row : row + 1], 0.0
-                )
-    accumulated.append(jnp.zeros((LANES - 3 * NSHELL, extent), jnp.float32))
-    gathered = jnp.concatenate(accumulated, axis=0)
-    pieces = []
-    for _ in range(3):
-        piece = gathered.astype(jnp.bfloat16)
-        gathered = gathered - piece.astype(jnp.float32)
-        pieces.append(piece)
-    shell_sums = matmul(
-        jnp.ones((SUBLANES, 3 * extent), jnp.bfloat16),
-        jnp.concatenate(pieces, axis=1),
-        ((1,), (1,)),
-    )
+        folded = jnp.sum(folded, axis=0, keepdims=True)
+        shift = LANES // 2
+        while shift >= NSHELL:
+            folded = folded + pltpu.roll(folded, shift, 1)
+            shift //= 2
+        shell_sums = jnp.where(row_lane // NSHELL == which, folded, shell_sums)
     out_ref[pl.ds(out_stride - 1, devices, stride=out_stride), :] = jnp.broadcast_to(
-        shell_sums[:1], (devices, LANES)
-    )
-
-    order = [(half, plane) for half in range(2) for plane in range(planes)]
-    backward = jnp.concatenate(
-        [averages[half, part, plane] for part in range(2) for half, plane in order], axis=0
-    )
-    back = matmul_split(split(backward), [high_ref[...], low_ref[...]])
+        shell_sums, (devices, LANES)
+    )
+
     offset = len(order) * rows
     blocks = {}
     for number, (half, plane) in enumerate(order):
@@ -332,7 +390,7 @@
     )
     turned = gathered.T
     left = jnp.concatenate([turned[: LANES // 2], turned[LANES // 2 :]], axis=1)
-    final = matmul_split(split(left), [high_ref[...], low_ref[...]])
+    final = matmul_rows(split(left), [high_ref[...], low_ref[...]])
     for half in range(halves):
         for plane in range(planes):
             real_at = ((half * parts + 0) * planes + plane) * own
@@ -341,6 +399,9 @@
             imag = final[imag_at : imag_at + own]
             maps_ref[half, 0, plane] = real[:, :extent] - imag[:, extent:]
             maps_ref[half, 1, plane] = real[:, extent:] + imag[:, :extent]
+
+
+small_grant = pltpu.CompilerParams(vmem_limit_bytes=16 * 1024 * 1024)
 
 
 def in_vmem(count):
@@ -377,12 +438,11 @@
     rows = shell_map.shape[1]
     extent = shell_map.shape[2]
     spectral = np.arange(extent)
-    smem = [pl.BlockSpec(memory_space=pltpu.SMEM)] * 3
 
     along_x = np.concatenate(
         cos_sin(spectral, np.arange(box_side) - box_side // 2, extent), axis=1
     )
-    x_high, x_low = split_table(along_x)
+    x_table = np.concatenate(split_table(along_x), axis=1)
     full = np.concatenate(cos_sin(spectral, spectral, extent), axis=1)
     y_high, y_low = split_table(full)
     half_rows = rows // 2
@@ -393,18 +453,34 @@
     ).reshape(-1)
     back_high, back_low = split_table(full[arrival])
 
+    smem = pl.BlockSpec(memory_space=pltpu.SMEM)
+    labels = pl.pallas_call(
+        functools.partial(label_kernel, rows, planes, extent),
+        out_shape=jax.ShapeDtypeStruct((devices, LANES), jnp.float32),
+        in_specs=[smem] * 3,
+        out_specs=in_vmem(1)[0],
+        compiler_params=small_grant,
+        cost_estimate=pl.CostEstimate(flops=140000000, bytes_accessed=0, transcendentals=0),
+    )(orientation, wedge_index, half_set)
     sent = pl.pallas_call(
         functools.partial(spread_kernel, rows),
         out_shape=jax.ShapeDtypeStruct((devices * (2 * planes * rows + 1), LANES), jnp.float32),
-        in_specs=smem + in_vmem(3),
+        in_specs=[smem] * 2 + in_vmem(3),
         out_specs=in_vmem(1)[0],
-    )(orientation, wedge_index, half_set, particles, x_high, x_low)
+        compiler_params=small_grant,
+    )(orientation, wedge_index, particles, x_table, labels)
     arrived = exchange(sent, devices)
     middle = pl.pallas_call(
         functools.partial(average_kernel, rows, planes),
         out_shape=jax.ShapeDtypeStruct((devices * (half_rows + 1), LANES), jnp.float32),
         in_specs=in_vmem(4),
         out_specs=in_vmem(1)[0],
+        scratch_shapes=[
+            pltpu.VMEM((planes * rows * NSHELL, extent), jnp.bfloat16),
+            pltpu.VMEM((devices, extent), jnp.bfloat16),
+            pltpu.VMEM((3 * planes * rows, planes * rows * NSHELL), jnp.float32),
+        ],
+        compiler_params=small_grant,
     )(arrived, shell_map, y_high, y_low)
     returned = exchange(middle, devices)
     half_maps, fsc = pl.pallas_call(
@@ -415,6 +491,7 @@
         ),
         in_specs=in_vmem(3),
         out_specs=tuple(in_vmem(2)),
+        compiler_params=small_grant,
     )(returned, back_high, back_low)
     return half_maps, fsc.reshape(NSHELL)
 

time: 44.9 us -> 39 us (0.87)
  Pallas kernels: 7.82 us -> 2.54 us
  blocking collectives: 34.2 us -> 33.5 us
    pallas_call x1, Pallas kernels: 3.52 us -> 1.18 us  [shards(): pl.pallas_call(functools.partial(average_kernel, rows, planes), out_shape...]
    pallas_call x1, Pallas kernels: 2.28 us -> 0.43 us  [shards(): pl.pallas_call(functools.partial(spread_kernel, rows), out_shape=jax.Shap...]
    pallas_call x1, Pallas kernels: 2.02 us -> 0.9 us  [shards(): pl.pallas_call(functools.partial(finish_kernel, rows), out_shape=(jax.Sha...]
    all_to_all x2, blocking collectives: 34.2 us -> 33.5 us  [exchange(): return lax.all_to_all(chunks, axes, 0, 0, tiled=True).reshape(values.shape)]
where the time goes in v3:
time: 39 us; the launch traced here: 38.8 us
  blocking collectives  33.5 us (86%)
  between operations  2.72 us (7%)
  Pallas kernels  2.54 us (7%)
    all_to_all x2, blocking collectives, exchange(): return lax.all_to_all(chunks, axes, 0, 0, tiled=True).reshape(values.shape)  33.5 us
    pallas_call x1, Pallas kernels, shards(): pl.pallas_call(functools.partial(average_kernel, rows, planes), out_shape...  1.18 us
    pallas_call x1, Pallas kernels, shards(): pl.pallas_call(functools.partial(finish_kernel, rows), out_shape=(jax.Sha...  0.9 us

profile of v3, /device:TPU:0, one launch (start us, length us, event | category | flops | bytes accessed | tf_op | source)
XLA Modules:
  0.0 38.8 jit_solution(14299026401383428523)
XLA Ops:
  0.6 0.0 copy-start.1
  0.6 0.0 copy-start
  2.7 0.0 copy-done.1
  2.7 0.0 copy-done
  2.7 0.4 %shard_map.114 = f32[1056,128]{1,0:T(8,128)S(1)} custom-call(s32[1]{0:T(128)S(6)} %copy.14.turn_ref, s32[1]{0:T(128)S(6)} %copy.15.wedge_ref, f32[1,2,2,128,128]{4,3,2,1,0:T(8,128)S(1)} %copy-done, bf16[256,512]{1,0:T(8,128)(2,1)S(1)} %copy-done.1, f32[32,128]{1,0:T(8,128)S(1)} %shard_map.113.label_ref), custom_call_target="tpu_custom_call" | custom-call | tf_op jit(solution)/shard_map/pallas_call | solution.py:465
  3.1 0.0 copy-start.4
  3.1 0.0 copy-start.5
  3.2 0.0 copy-start.6
  3.2 23.0 %all_to_all.10 = f32[32,33,1,128]{3,2,1,0:T(1,128)S(1)} all-to-all(f32[32,33,1,128]{3,2,1,0:T(1,128)S(1)} %bitcast.5), channel_id=1, replica_groups=mesh['px'=8,'py'=4] {'px','py'}, dimensions={0} | all-to-all | bytes 1081344 | tf_op jit(solution)/shard_map/all_to_all | solution.py:413
  26.2 0.0 copy-done.4
  26.2 0.0 copy-done.5
  26.2 0.0 copy-done.6
  26.2 0.0 copy-start.2
  26.2 0.0 copy-start.3
  26.3 1.2 %shard_map.115 = f32[160,128]{1,0:T(8,128)S(1)} custom-call(f32[1056,128]{1,0:T(8,128)S(1)} %bitcast.6, s32[2,8,256]{2,1,0:T(8,128)S(1)} %copy-done.6, bf16[256,512]{1,0:T(8,128)(2,1)S(1)} %copy-done.5, bf16[256,512]{1,0:T(8,128)(2,1)S(1)} %copy-done.4), custom_call_target="tpu_custom_call" | custom-call | tf_op jit(solution)/shard_map/pallas_call | solution.py:473
  27.4 10.4 %all_to_all.11 = f32[32,5,1,128]{3,2,1,0:T(1,128)S(1)} all-to-all(f32[32,5,1,128]{3,2,1,0:T(1,128)S(1)} %bitcast.7), channel_id=1, replica_groups=mesh['px'=8,'py'=4] {'px','py'}, dimensions={0} | all-to-all | bytes 163840 | tf_op jit(solution)/shard_map/all_to_all | solution.py:413
  37.9 0.0 copy-done.2
  37.9 0.0 copy-done.3
  37.9 0.9 %shard_map.116 = (f32[2,2,2,8,256]{4,3,2,1,0:T(8,128)}, f32[1,32]{1,0:T(1,128)}) custom-call(f32[160,128]{1,0:T(8,128)S(1)} %bitcast.8, bf16[256,512]{1,0:T(8,128)(2,1)S(1)} %copy-done.3, bf16[256,512]{1,0:T(8,128)(2,1)S(1)} %copy-done.2), custom_call_target="tpu_custom_call" | custom-call | tf_op jit(solution)/shard_map/pallas_call | solution.py:486
  (1 shorter events, 0.0 us)
Async XLA Ops:
  0.6 2.0 %copy-start.1 = (bf16[256,512]{1,0:T(8,128)(2,1)S(1)}, bf16[256,512]{1,0:T(8,128)(2,1)}, u32[]{:S(2)}) copy-start(bf16[256,512]{1,0:T(8,128)(2,1)} %constant.10.clone.table_ref) | copy-start | bytes 786436
  0.6 2.0 %copy-start = (f32[1,2,2,128,128]{4,3,2,1,0:T(8,128)S(1)}, f32[1,2,2,128,128]{4,3,2,1,0:T(8,128)}, u32[]{:S(2)}) copy-start(f32[1,2,2,128,128]{4,3,2,1,0:T(8,128)} %source_ref.1) | copy-start | bytes 786436
  3.1 23.1 %copy-start.4 = (bf16[256,512]{1,0:T(8,128)(2,1)S(1)}, bf16[256,512]{1,0:T(8,128)(2,1)}, u32[]{:S(2)}) copy-start(bf16[256,512]{1,0:T(8,128)(2,1)} %constant.12.clone.low_ref) | copy-start | bytes 786436
  3.1 23.1 %copy-start.5 = (bf16[256,512]{1,0:T(8,128)(2,1)S(1)}, bf16[256,512]{1,0:T(8,128)(2,1)}, u32[]{:S(2)}) copy-start(bf16[256,512]{1,0:T(8,128)(2,1)} %constant.11.clone.high_ref) | copy-start | bytes 786436
  3.2 23.1 %copy-start.6 = (s32[2,8,256]{2,1,0:T(8,128)S(1)}, s32[2,8,256]{2,1,0:T(8,128)}, u32[]{:S(2)}) copy-start(s32[2,8,256]{2,1,0:T(8,128)} %shell_ref.1) | copy-start | bytes 49156
  26.2 11.6 %copy-start.2 = (bf16[256,512]{1,0:T(8,128)(2,1)S(1)}, bf16[256,512]{1,0:T(8,128)(2,1)}, u32[]{:S(2)}) copy-start(bf16[256,512]{1,0:T(8,128)(2,1)} %constant.14.clone.low_ref) | copy-start | bytes 786436
  26.2 11.6 %copy-start.3 = (bf16[256,512]{1,0:T(8,128)(2,1)S(1)}, bf16[256,512]{1,0:T(8,128)(2,1)}, u32[]{:S(2)}) copy-start(bf16[256,512]{1,0:T(8,128)(2,1)} %constant.13.clone.high_ref) | copy-start | bytes 786436
